TPU v7x, 256 devices: a whole 4x4x8 slice. The times are simulated.
256 devices in a mesh: leaf: 64 (over x, z, core), front: 4 (over y).
Axes of the slice: x: 4, y: 4, z: 8, core: 2. Of those that a mesh axis runs over, the one named last changes fastest.
Arguments:
- leaf_update: float32 [65536, 1024], P('leaf'), as said below
- separator_rows_1: float32 [16384, 1536], P(('leaf', 'front')), as said below
- remaining_rows_1: float32 [32768, 1536], P(('leaf', 'front'))
- separator_rows_2: float32 [8192, 1536], P(('leaf', 'front')), as said below
- remaining_rows_2: float32 [16384, 1536], P(('leaf', 'front'))
- separator_rows_3: float32 [4096, 1536], P(('leaf', 'front')), as said below
- remaining_rows_3: float32 [8192, 1536], P(('leaf', 'front'))
- child_map_1: int32 [64, 8], replicated, may hold values from 0 to 11, as said below
- child_map_2: int32 [32, 8], replicated, may hold values from 0 to 11, as said below
- child_map_3: int32 [16, 8], replicated, may hold values from 0 to 11, as said below
Outputs:
- pivot_factor_1: float32 [16384, 512], P(('leaf', 'front'))
- below_factor_1: float32 [32768, 512], P(('leaf', 'front'))
- pivot_factor_2: float32 [8192, 512], P(('leaf', 'front'))
- below_factor_2: float32 [16384, 512], P(('leaf', 'front'))
- pivot_factor_3: float32 [4096, 512], P(('leaf', 'front'))
- below_factor_3: float32 [8192, 512], P(('leaf', 'front'))
Inputs may be any that keep to these rules, and one draw needn't show every extreme that they name: `child_map_1`: each row lists 8 distinct parent tiles in increasing order, the last one always 12 - 1. `child_map_2`: each row lists 8 distinct parent tiles in increasing order, the last one always 12 - 1. `child_map_3`: each row lists 8 distinct parent tiles in increasing order, the last one always 12 - 1. `leaf_update`: each block is symmetric positive definite, diagonal between 0.5 and 2, off-diagonal entries of magnitude about 0.008, smallest eigenvalue about 0.1 or more. Each front, separator_rows_1 above remaining_rows_1, is symmetric positive definite, diagonal between 2 and 4, off-diagonal entries of magnitude about 0.03, smallest eigenvalue about 0.35 or more. Each front, separator_rows_2 above remaining_rows_2, is symmetric positive definite, diagonal between 2 and 4, off-diagonal entries of magnitude about 0.03, smallest eigenvalue about 0.35 or more. Each front, separator_rows_3 above remaining_rows_3, is symmetric positive definite, diagonal between 2 and 4, off-diagonal entries of magnitude about 0.03, smallest eigenvalue about 0.35 or more.
All inputs are finite; a program needn't handle non-finite values.
Results may differ from a plain program's by a relative error of at most 0.0003.
Values sent between devices are 32-bit elements; how exact they have to be, the bound alone decides.
No kernel may reach another device: no remote copies, remote signals or barrier semaphores. Data moves between devices by JAX's collectives and lax.ppermute only.
A program may use at most 128 MiB of HBM per device.

v0:
```python
import jax
import jax.numpy as jnp
from jax import lax
from jax.sharding import PartitionSpec as P

TILE = 128
SEP = 512
UPD = 1024
NF = 1536
NT = 12
UT = 8


def from_partner(block, axis, stride):
    count = lax.axis_size(axis)
    route = []
    for low in range(count):
        high = low | 1 << stride
        if high != low and high < count:
            route += [(low, high), (high, low)]
    return lax.ppermute(block, axis, route)


def collect(pieces, depth_count):
    gathered = lax.all_gather(pieces, "front", axis=0, tiled=True)
    leaf_place = lax.axis_index("leaf")
    for bit_number in range(depth_count):
        partner = from_partner(gathered, "leaf", bit_number)
        on_high = leaf_place >> bit_number & 1 == 1
        gathered = jnp.where(
            on_high,
            jnp.concatenate([partner, gathered], axis=0),
            jnp.concatenate([gathered, partner], axis=0),
        )
    return gathered


def owned_rows(position, group_count):
    sep_count = SEP // group_count
    upd_count = UPD // group_count
    sep_index = position * sep_count + jnp.arange(sep_count, dtype=jnp.int32)
    upd_index = SEP + position * upd_count + jnp.arange(upd_count, dtype=jnp.int32)
    return jnp.concatenate([sep_index, upd_index])


def locate(tile_map, targets):
    tile_of = targets // TILE
    offset = targets % TILE
    matches = tile_map[None, :] == tile_of[:, None]
    present = jnp.any(matches, axis=1)
    slot_ids = jnp.arange(tile_map.shape[0], dtype=jnp.int32)
    source = jnp.sum(jnp.where(matches, slot_ids[None, :], 0), axis=1)
    return (source * TILE + offset, present)


def select_rows(full_update, tile_map, targets):
    source, present = locate(tile_map, targets)
    return jnp.where(present[:, None], jnp.take(full_update, source, axis=0), 0.0)


def expand_columns(row_block, tile_map):
    placing = (tile_map[:, None] == jnp.arange(NT, dtype=jnp.int32)[None, :]).astype(jnp.float32)
    tiled = row_block.reshape(row_block.shape[0], UT, TILE)
    placed = jnp.einsum("rut,un->rnt", tiled, placing, precision=lax.Precision.HIGHEST)
    return placed.reshape(row_block.shape[0], NF)


def body(
    leaf_update,
    separator_rows_1,
    remaining_rows_1,
    separator_rows_2,
    remaining_rows_2,
    separator_rows_3,
    remaining_rows_3,
    child_map_1,
    child_map_2,
    child_map_3,
):
    leaf_place = lax.axis_index("leaf")
    front_place = lax.axis_index("front")
    front_count = lax.axis_size("front")
    child_full = leaf_update
    sections = (
        (separator_rows_1, remaining_rows_1, child_map_1),
        (separator_rows_2, remaining_rows_2, child_map_2),
        (separator_rows_3, remaining_rows_3, child_map_3),
    )
    results = []
    for level_number in range(1, 4):
        sep_part, upd_part, child_maps = sections[level_number - 1]
        group_count = front_count * 2**level_number
        sep_count = SEP // group_count
        upd_count = UPD // group_count
        pair_bit = level_number - 1
        child_front = leaf_place >> pair_bit
        sibling_front = child_front ^ 1
        position = leaf_place % 2**level_number * front_count + front_place
        own_map = lax.dynamic_index_in_dim(child_maps, child_front, 0, keepdims=False)
        targets = owned_rows(position, group_count)
        sibling_map = lax.dynamic_index_in_dim(child_maps, sibling_front, 0, keepdims=False)
        sibling_full = from_partner(child_full, "leaf", pair_bit)
        sibling_block = select_rows(sibling_full, sibling_map, targets)
        own_term = expand_columns(select_rows(child_full, own_map, targets), own_map)
        sibling_term = expand_columns(sibling_block, sibling_map)
        is_odd = child_front & 1 == 1
        earlier_term = jnp.where(is_odd, sibling_term, own_term)
        later_term = jnp.where(is_odd, own_term, sibling_term)
        front_rows = jnp.concatenate([sep_part, upd_part], axis=0) + earlier_term + later_term
        panel_all = collect(front_rows[:, :SEP], level_number)
        blocks = panel_all.reshape(group_count, sep_count + upd_count, SEP)
        pivot_block = blocks[:, :sep_count].reshape(SEP, SEP)
        lower_block = blocks[:, sep_count:].reshape(UPD, SEP)
        diag_factor = jnp.linalg.cholesky(pivot_block)
        solved_all = lax.linalg.triangular_solve(
            diag_factor, lower_block, left_side=False, lower=True, transpose_a=True
        )
        solved_own = lax.dynamic_slice_in_dim(solved_all, position * upd_count, upd_count, 0)
        results.append(lax.dynamic_slice_in_dim(diag_factor, position * sep_count, sep_count, 0))
        results.append(solved_own)
        if level_number < 3:
            update_own = front_rows[sep_count:, SEP:] - jnp.dot(
                solved_own, solved_all.T, precision=lax.Precision.HIGHEST
            )
            child_full = collect(update_own, level_number)
    return (results[0], results[1], results[2], results[3], results[4], results[5])


def solution(mesh):
    in_specs = (
        P("leaf", None),
        P(("leaf", "front"), None),
        P(("leaf", "front"), None),
        P(("leaf", "front"), None),
        P(("leaf", "front"), None),
        P(("leaf", "front"), None),
        P(("leaf", "front"), None),
        P(),
        P(),
        P(),
    )
    out_specs = (
        P(("leaf", "front"), None),
        P(("leaf", "front"), None),
        P(("leaf", "front"), None),
        P(("leaf", "front"), None),
        P(("leaf", "front"), None),
        P(("leaf", "front"), None),
    )
    return jax.shard_map(body, mesh=mesh, in_specs=in_specs, out_specs=out_specs, check_vma=False)
```

profile of v0, /device:TPU:1, one launch (start us, length us, event | category | flops | bytes accessed | tf_op | source)
XLA Modules:
  0.0 1112.1 jit_solution(10254888534688105837)
XLA Ops:
  7.2 3.3 collective-permute-start
  11.8 3.5 gather_fusion.1
  17.7 3.5 gather_fusion
  25.7 30.1 %all-gather.4.cloned.1.call-done = f32[768,512]{1,0:T(8,128)} async-done(((f32[192,512]{1,0:T(8,128)}), f32[768,512]{1,0:T(8,128)}) %all-gather.4.cloned.1.call-update) | async-done | bytes 1572880 | tf_op jit(solution)/shard_map/all_gather | solution.py:25
  66.7 11.7 %cholesky.374 = f32[128,128]{1,0:T(8,128)S(1)} custom-call(f32[128,128]{1,0:T(8,128)S(1)} %cholesky.586), custom_call_target="Cholesky" | custom-call | tf_op jit(solution)/shard_map/jit(cholesky)/cholesky | solution.py:114
  78.6 9.8 custom-call.31
  90.9 11.7 %cholesky.393 = f32[128,128]{1,0:T(8,128)S(1)} custom-call(f32[128,128]{1,0:T(8,128)S(1)} %cholesky.590), custom_call_target="Cholesky" | custom-call | tf_op jit(solution)/shard_map/jit(cholesky)/cholesky | solution.py:114
  102.7 10.0 custom-call.32
  114.2 11.7 %cholesky.414 = f32[128,128]{1,0:T(8,128)S(1)} custom-call(f32[128,128]{1,0:T(8,128)S(1)} %cholesky.595), custom_call_target="Cholesky" | custom-call | tf_op jit(solution)/shard_map/jit(cholesky)/cholesky | solution.py:114
  126.0 9.8 custom-call.33
  137.2 12.1 %cholesky.431 = f32[128,128]{1,0:T(8,128)S(1)} custom-call(f32[128,128]{1,0:T(8,128)S(1)} %convolution_subtract_fusion.10), custom_call_target="Cholesky" | custom-call | tf_op jit(solution)/shard_map/jit(cholesky)/cholesky | solution.py:114
  156.1 11.6 %while.6 = (s32[]{:T(128)}, f32[512,512]{1,0:T(8,128)}, s32[4,2]{0,1:T(2,128)S(1)}, f32[4,128,128]{2,1,0:T(8,128)S(1)}, s32[]{:T(128)}) while((s32[]{:T(128)}, f32[512,512]{1,0:T(8,128)}, s32[4,2]{0,1:T(2,128)S(1)}, f32[4,128,128]{2,1,0:T(8,128)S(1)}, s32[]{:T(128)}) %tuple.112), condition=%wide.while_cond, body=%wide.while_body.sunk | while | flops 2 | bytes 131189 | solution.py:115
  167.7 39.3 %custom-call.34 = f32[4,128,128]{1,2,0:T(8,128)S(1)} custom-call(f32[4,128,128]{2,1,0:T(8,128)S(1)} %get-tuple-element.31), custom_call_target="InvertDiagBlocksLowerTriangular" | custom-call | tf_op jit(solution)/shard_map/triangular_solve/custom-call.3 | solution.py:115
  213.6 3.7 fusion
  222.2 33.3 %all-gather.6.cloned.1.call-done = f32[512,1024]{1,0:T(8,128)} async-done(((f32[128,1024]{1,0:T(8,128)}), f32[512,1024]{1,0:T(8,128)}) %all-gather.6.cloned.1.call-update) | async-done | bytes 2097168 | tf_op jit(solution)/shard_map/all_gather | solution.py:25
  256.3 4.0 collective-permute-done.2
  260.3 5.1 maximum_select_fusion
  270.9 86.6 %collective-permute-done.3 = f32[1024,1024]{1,0:T(8,128)} collective-permute-done((f32[1024,1024]{1,0:T(8,128)}, f32[1024,1024]{1,0:T(8,128)}, u32[]{:S(2)}, u32[]{:S(2)}) %collective-permute-start.3) | collective-permute-done | bytes 4194336 | tf_op jit(solution)/shard_map/ppermute | solution.py:21
  362.2 10.7 all_gather.17
  372.9 4.8 collective-permute-start.4
  381.1 34.3 %collective-permute-done.5 = f32[768,512]{1,0:T(8,128)S(1)} collective-permute-done((f32[768,512]{1,0:T(8,128)S(1)}, f32[768,512]{1,0:T(8,128)S(1)}, u32[]{:S(2)}, u32[]{:S(2)}) %collective-permute-start.5) | collective-permute-done | bytes 1572896 | tf_op jit(solution)/shard_map/ppermute | solution.py:21
  419.8 11.7 %cholesky.446 = f32[128,128]{1,0:T(8,128)S(1)} custom-call(f32[128,128]{1,0:T(8,128)S(1)} %cholesky.599), custom_call_target="Cholesky" | custom-call | tf_op jit(solution)/shard_map/jit(cholesky)/cholesky | solution.py:114
  431.6 9.8 custom-call.35
  444.0 11.7 %cholesky.465 = f32[128,128]{1,0:T(8,128)S(1)} custom-call(f32[128,128]{1,0:T(8,128)S(1)} %cholesky.603), custom_call_target="Cholesky" | custom-call | tf_op jit(solution)/shard_map/jit(cholesky)/cholesky | solution.py:114
  455.7 10.2 custom-call.36
  467.5 11.7 %cholesky.486 = f32[128,128]{1,0:T(8,128)S(1)} custom-call(f32[128,128]{1,0:T(8,128)S(1)} %cholesky.608), custom_call_target="Cholesky" | custom-call | tf_op jit(solution)/shard_map/jit(cholesky)/cholesky | solution.py:114
  479.2 9.8 custom-call.37
  490.5 11.9 %cholesky.503 = f32[128,128]{1,0:T(8,128)S(1)} custom-call(f32[128,128]{1,0:T(8,128)S(1)} %convolution_subtract_fusion.9), custom_call_target="Cholesky" | custom-call | tf_op jit(solution)/shard_map/jit(cholesky)/cholesky | solution.py:114
  509.1 11.6 %while.7 = (s32[]{:T(128)}, f32[512,512]{1,0:T(8,128)}, s32[4,2]{0,1:T(2,128)S(1)}, f32[4,128,128]{2,1,0:T(8,128)S(1)}, s32[]{:T(128)}) while((s32[]{:T(128)}, f32[512,512]{1,0:T(8,128)}, s32[4,2]{0,1:T(2,128)S(1)}, f32[4,128,128]{2,1,0:T(8,128)S(1)}, s32[]{:T(128)}) %tuple.127), condition=%wide.while_cond.clone, body=%wide.while_body.clone.sunk | while | flops 2 | bytes 131189 | solution.py:115
  520.7 39.3 %custom-call.38 = f32[4,128,128]{1,2,0:T(8,128)S(1)} custom-call(f32[4,128,128]{2,1,0:T(8,128)S(1)} %get-tuple-element.32), custom_call_target="InvertDiagBlocksLowerTriangular" | custom-call | tf_op jit(solution)/shard_map/triangular_solve/custom-call.3 | solution.py:115
  566.6 3.7 fusion.6
  574.4 26.1 %all-gather.8.cloned.1.call-done = f32[256,1024]{1,0:T(8,128)} async-done(((f32[64,1024]{1,0:T(8,128)}), f32[256,1024]{1,0:T(8,128)}) %all-gather.8.cloned.1.call-update) | async-done | bytes 1048592 | tf_op jit(solution)/shard_map/all_gather | solution.py:25
  608.2 45.6 %collective-permute-done.7 = f32[512,1024]{1,0:T(8,128)S(1)} collective-permute-done((f32[512,1024]{1,0:T(8,128)S(1)}, f32[512,1024]{1,0:T(8,128)S(1)}, u32[]{:S(2)}, u32[]{:S(2)}) %collective-permute-start.7) | collective-permute-done | bytes 2097184 | tf_op jit(solution)/shard_map/ppermute | solution.py:21
  662.4 176.2 %collective-permute-done.8 = f32[1024,1024]{1,0:T(8,128)} collective-permute-done((f32[1024,1024]{1,0:T(8,128)}, f32[1024,1024]{1,0:T(8,128)}, u32[]{:S(2)}, u32[]{:S(2)}) %collective-permute-start.8) | collective-permute-done | bytes 4194336 | tf_op jit(solution)/shard_map/ppermute | solution.py:21
  842.6 10.9 all_gather.19
  853.5 3.5 collective-permute-start.9
  858.5 18.7 %collective-permute-done.10 = f32[384,512]{1,0:T(8,128)S(1)} collective-permute-done((f32[384,512]{1,0:T(8,128)S(1)}, f32[384,512]{1,0:T(8,128)S(1)}, u32[]{:S(2)}, u32[]{:S(2)}) %collective-permute-start.10) | collective-permute-done | bytes 786464 | tf_op jit(solution)/shard_map/ppermute | solution.py:21
  885.1 62.8 %collective-permute-done.11 = f32[768,512]{1,0:T(8,128)S(1)} collective-permute-done((f32[768,512]{1,0:T(8,128)S(1)}, f32[768,512]{1,0:T(8,128)S(1)}, u32[]{:S(2)}, u32[]{:S(2)}) %collective-permute-start.11) | collective-permute-done | bytes 1572896 | tf_op jit(solution)/shard_map/ppermute | solution.py:21
  952.3 11.7 %cholesky.518 = f32[128,128]{1,0:T(8,128)S(1)} custom-call(f32[128,128]{1,0:T(8,128)S(1)} %cholesky.612), custom_call_target="Cholesky" | custom-call | tf_op jit(solution)/shard_map/jit(cholesky)/cholesky | solution.py:114
  964.2 9.8 custom-call.39
  976.5 11.7 %cholesky.537 = f32[128,128]{1,0:T(8,128)S(1)} custom-call(f32[128,128]{1,0:T(8,128)S(1)} %cholesky.616), custom_call_target="Cholesky" | custom-call | tf_op jit(solution)/shard_map/jit(cholesky)/cholesky | solution.py:114
  988.2 9.9 custom-call.40
  999.8 11.7 %cholesky.558 = f32[128,128]{1,0:T(8,128)S(1)} custom-call(f32[128,128]{1,0:T(8,128)S(1)} %cholesky.621), custom_call_target="Cholesky" | custom-call | tf_op jit(solution)/shard_map/jit(cholesky)/cholesky | solution.py:114
  1011.5 9.8 custom-call.41
  1022.8 11.9 %cholesky.575 = f32[128,128]{1,0:T(8,128)S(1)} custom-call(f32[128,128]{1,0:T(8,128)S(1)} %convolution_subtract_fusion.8), custom_call_target="Cholesky" | custom-call | tf_op jit(solution)/shard_map/jit(cholesky)/cholesky | solution.py:114
  1041.6 11.5 %while.8 = (s32[]{:T(128)}, f32[512,512]{1,0:T(8,128)}, s32[4,2]{0,1:T(2,128)S(1)}, f32[4,128,128]{2,1,0:T(8,128)S(1)}, s32[]{:T(128)}) while((s32[]{:T(128)}, f32[512,512]{1,0:T(8,128)}, s32[4,2]{0,1:T(2,128)S(1)}, f32[4,128,128]{2,1,0:T(8,128)S(1)}, s32[]{:T(128)}) %tuple.128), condition=%wide.while_cond.clone.1, body=%wide.while_body.clone.1.sunk | while | flops 2 | bytes 131189 | solution.py:115
  1053.0 39.3 %custom-call.42 = f32[4,128,128]{1,2,0:T(8,128)S(1)} custom-call(f32[4,128,128]{2,1,0:T(8,128)S(1)} %get-tuple-element.33), custom_call_target="InvertDiagBlocksLowerTriangular" | custom-call | tf_op jit(solution)/shard_map/triangular_solve/custom-call.3 | solution.py:115
  1098.8 3.6 fusion.12
  (250 shorter events, 166.8 us)
Async XLA Ops:
  7.2 48.7 %all-gather.4.cloned.1.call-start = ((), (), s32[]{:S(2)}) async-start(), calls=%async_computation | async-start | bytes 1966080 | tf_op jit(solution)/shard_map/all_gather | solution.py:25
  7.2 10.5 collective-permute-start
  21.5 1.1 copy-start.6
  21.5 1.2 copy-start.8
  23.9 1.0 copy-start.3
  25.7 229.8 %all-gather.6.cloned.1.call-start = ((), (), s32[]{:S(2)}) async-start(), calls=%async_computation.1 | async-start | bytes 2621440 | tf_op jit(solution)/shard_map/all_gather | solution.py:25
  55.9 4.4 collective-permute-start.1
  65.7 1.0 copy-start
  218.2 0.7 copy-start.4
  222.1 378.4 %all-gather.8.cloned.1.call-start = ((), (), s32[]{:S(2)}) async-start(), calls=%async_computation.2 | async-start | bytes 1310720 | tf_op jit(solution)/shard_map/all_gather | solution.py:25
  255.5 4.8 collective-permute-start.2
  265.4 92.1 %collective-permute-start.3 = (f32[1024,1024]{1,0:T(8,128)}, f32[1024,1024]{1,0:T(8,128)}, u32[]{:S(2)}, u32[]{:S(2)}) collective-permute-start(f32[1024,1024]{1,0:T(8,128)} %maximum_select_fusion), channel_id=1, source_target_pairs={{0,8},{8,0},{4,12},{12,4},{16,24},{24,16},{20,28},{28,20},{32,40},... | collective-permute-start | bytes 12582920 | tf_op jit(solution)/shard_map/ppermute | solution.py:21
  360.6 1.0 copy-start.7
  360.6 1.0 copy-start.10
  362.2 15.5 %copy-start.5 = (f32[96,1536]{1,0:T(8,128)}, f32[96,1536]{1,0:T(8,128)S(1)}, u32[]{:S(2)}) copy-start(f32[96,1536]{1,0:T(8,128)S(1)} %bitcast_add_fusion.5) | copy-start | bytes 1769476
  372.9 6.7 collective-permute-start.4
  379.7 35.7 %collective-permute-start.5 = (f32[768,512]{1,0:T(8,128)S(1)}, f32[768,512]{1,0:T(8,128)S(1)}, u32[]{:S(2)}, u32[]{:S(2)}) collective-permute-start(f32[768,512]{1,0:T(8,128)S(1)} %maximum_select_fusion.6), channel_id=1, source_target_pairs={{0,8},{8,0},{4,12},{12,4},{16,24},{24,16},{20,28},{28,20},{32,40},... | collective-permute-start | bytes 4718600 | tf_op jit(solution)/shard_map/ppermute | solution.py:21
  418.8 1.0 copy-start.1
  600.5 4.5 collective-permute-start.6
  606.8 51.6 %copy-start.12 = (s32[16,8]{0,1:T(8,128)S(1)}, s32[16,8]{0,1:T(8,128)}, u32[]{:S(2)}) copy-start(s32[16,8]{0,1:T(8,128)} %param.28) | copy-start | bytes 1540
  606.8 46.9 %collective-permute-start.7 = (f32[512,1024]{1,0:T(8,128)S(1)}, f32[512,1024]{1,0:T(8,128)S(1)}, u32[]{:S(2)}, u32[]{:S(2)}) collective-permute-start(f32[512,1024]{1,0:T(8,128)S(1)} %maximum_select_fusion.5), channel_id=1, source_target_pairs={{0,8},{8,0},{4,12},{12,4},{16,24},{24,16},{20,28},{28,20},{32,40},... | collective-permute-start | bytes 6291464 | tf_op jit(solution)/shard_map/ppermute | solution.py:21
  656.1 182.5 %collective-permute-start.8 = (f32[1024,1024]{1,0:T(8,128)}, f32[1024,1024]{1,0:T(8,128)}, u32[]{:S(2)}, u32[]{:S(2)}) collective-permute-start(f32[1024,1024]{1,0:T(8,128)} %maximum_select_fusion.1), channel_id=1, source_target_pairs={{0,16},{16,0},{4,20},{20,4},{8,24},{24,8},{12,28},{28,12},{32,48},... | collective-permute-start | bytes 12582920 | tf_op jit(solution)/shard_map/ppermute | solution.py:21
  841.6 0.9 copy-start.9
  841.6 1.0 copy-start.11
  853.5 4.9 collective-permute-start.9
  858.4 18.8 %collective-permute-start.10 = (f32[384,512]{1,0:T(8,128)S(1)}, f32[384,512]{1,0:T(8,128)S(1)}, u32[]{:S(2)}, u32[]{:S(2)}) collective-permute-start(f32[384,512]{1,0:T(8,128)S(1)} %maximum_select_fusion.8), channel_id=1, source_target_pairs={{0,8},{8,0},{4,12},{12,4},{16,24},{24,16},{20,28},{28,20},{32,40},... | collective-permute-start | bytes 2359304 | tf_op jit(solution)/shard_map/ppermute | solution.py:21
  877.5 70.5 %collective-permute-start.11 = (f32[768,512]{1,0:T(8,128)S(1)}, f32[768,512]{1,0:T(8,128)S(1)}, u32[]{:S(2)}, u32[]{:S(2)}) collective-permute-start(f32[768,512]{1,0:T(8,128)S(1)} %maximum_select_fusion.7), channel_id=1, source_target_pairs={{0,16},{16,0},{4,20},{20,4},{8,24},{24,8},{12,28},{28,12},{32,48},... | collective-permute-start | bytes 4718600 | tf_op jit(solution)/shard_map/ppermute | solution.py:21
  951.3 1.0 copy-start.2
Sparse Core Ops, SparseCore 0:
  25.8 30.0 all-gather.3
  222.2 33.1 all-gather.5
  574.6 25.8 all-gather.7
where the time goes:
time: 1120 us; the launch traced here: 1110 us
  waiting for transfers between devices  528 us (47%)
  other arithmetic  382 us (34%)
  local copies, waits for them, and re-layouts  74.5 us (7%)
  matrix products  59 us (5%)
  starting transfers between devices  24.1 us (2%)
  between operations  22.8 us (2%)
  blocking collectives  21.5 us (2%)
    ppermute x12, waiting for transfers between devices, from_partner(): return lax.ppermute(block, axis, route)  438 us
    another operation x45, other arithmetic, body(): diag_factor = jnp.linalg.cholesky(pivot_block)  238 us
    another operation x10, other arithmetic, body(): lax.linalg.triangular_solve(diag_factor, lower_block, left_side=False, lo...  123 us
    all_gather x3, waiting for transfers between devices, collect(): gathered = lax.all_gather(pieces, 'front', axis=0, tiled=True)  89.5 us
    another operation x40, local copies, waits for them, and re-layouts, body(): lax.linalg.triangular_solve(diag_factor, lower_block, left_side=False, lo...  34.4 us
    another operation x21, matrix products, body(): lax.linalg.triangular_solve(diag_factor, lower_block, left_side=False, lo...  32.4 us
    ppermute x12, starting transfers between devices, from_partner(): return lax.ppermute(block, axis, route)  24 us
  transfers between devices with their start and end apart: 15, of which 15 were waited for; matrix products, arithmetic and copies ran while one was open for 2% of the time, Pallas kernels for 0%

commit v1 on v0

--- a/solution.py
+++ b/solution.py
@@ -22,7 +22,11 @@
 
 
 def collect(pieces, depth_count):
-    gathered = lax.all_gather(pieces, "front", axis=0, tiled=True)
+    tell_layers_all_over_axis = lambda payload, axis_name, dim_no: jnp.concatenate(
+        jax.lax.all_to_all(jnp.stack(jax.lax.axis_size(axis_name) * [payload]), axis_name, 0, 0),
+        axis=dim_no,
+    )
+    gathered = tell_layers_all_over_axis(pieces, "front", 0)
     leaf_place = lax.axis_index("leaf")
     for bit_number in range(depth_count):
         partner = from_partner(gathered, "leaf", bit_number)

time: 1120 us -> 1080 us (0.964)
  waiting for transfers between devices: 528 us -> 435 us
  blocking collectives: 21.5 us -> 89.9 us
  between operations: 22.8 us -> 9.94 us
    all_to_all x0 -> x5, blocking collectives: none -> 89.9 us  [collect(): jax.lax.all_to_all(jnp.stack(jax.lax.axis_size(axis_name) * [payload]), a...]
    all_gather x3 -> x0, waiting for transfers between devices: 89.5 us -> none  [collect(): gathered = lax.all_gather(pieces, 'front', axis=0, tiled=True)]
    all_gather x2 -> x0, blocking collectives: 21.5 us -> none  [collect(): gathered = lax.all_gather(pieces, 'front', axis=0, tiled=True)]
  transfers between devices with their start and end apart: 15 -> 12, of which waited for: 15 -> 12; matrix products, arithmetic and copies ran while one was open for 2% -> 2% of each run, Pallas kernels for 0% -> 0%
where the time goes in v1:
time: 1080 us; the launch traced here: 1070 us
  waiting for transfers between devices  435 us (40%)
  other arithmetic  375 us (35%)
  blocking collectives  89.9 us (8%)
  local copies, waits for them, and re-layouts  72.8 us (7%)
  matrix products  57.6 us (5%)
  starting transfers between devices  26.9 us (2%)
    ppermute x12, waiting for transfers between devices, from_partner(): return lax.ppermute(block, axis, route)  435 us
    another operation x45, other arithmetic, body(): diag_factor = jnp.linalg.cholesky(pivot_block)  238 us
    another operation x10, other arithmetic, body(): lax.linalg.triangular_solve(diag_factor, lower_block, left_side=False, lo...  123 us
    all_to_all x5, blocking collectives, collect(): jax.lax.all_to_all(jnp.stack(jax.lax.axis_size(axis_name) * [payload]), a...  89.9 us
    another operation x40, local copies, waits for them, and re-layouts, body(): lax.linalg.triangular_solve(diag_factor, lower_block, left_side=False, lo...  34.4 us
    another operation x21, matrix products, body(): lax.linalg.triangular_solve(diag_factor, lower_block, left_side=False, lo...  32.4 us
    ppermute x12, starting transfers between devices, from_partner(): return lax.ppermute(block, axis, route)  26.9 us
  transfers between devices with their start and end apart: 12, of which 12 were waited for; matrix products, arithmetic and copies ran while one was open for 2% of the time, Pallas kernels for 0%

profile of v1, /device:TPU:1, one launch (start us, length us, event | category | flops | bytes accessed | tf_op | source)
XLA Modules:
  0.0 1068.0 jit_solution(13864724606370952503)
XLA Ops:
  0.6 3.3 collective-permute-start
  5.2 3.5 gather_fusion.1
  11.1 3.5 gather_fusion
  17.5 22.8 %all_to_all.25 = f32[4,192,512]{2,1,0:T(8,128)S(1)} all-to-all(f32[4,192,512]{2,1,0:T(8,128)S(1)} %stack.10), channel_id=1, replica_groups=mesh['leaf'=64,'front'=4] {'front'}, dimensions={0} | all-to-all | bytes 3145728 | tf_op jit(solution)/shard_map/all_to_all | solution.py:26
  49.3 11.7 %cholesky.374 = f32[128,128]{1,0:T(8,128)S(1)} custom-call(f32[128,128]{1,0:T(8,128)S(1)} %cholesky.586), custom_call_target="Cholesky" | custom-call | tf_op jit(solution)/shard_map/jit(cholesky)/cholesky | solution.py:118
  61.2 9.8 custom-call.31
  73.5 11.7 %cholesky.393 = f32[128,128]{1,0:T(8,128)S(1)} custom-call(f32[128,128]{1,0:T(8,128)S(1)} %cholesky.590), custom_call_target="Cholesky" | custom-call | tf_op jit(solution)/shard_map/jit(cholesky)/cholesky | solution.py:118
  85.3 10.2 custom-call.32
  97.1 11.7 %cholesky.414 = f32[128,128]{1,0:T(8,128)S(1)} custom-call(f32[128,128]{1,0:T(8,128)S(1)} %cholesky.595), custom_call_target="Cholesky" | custom-call | tf_op jit(solution)/shard_map/jit(cholesky)/cholesky | solution.py:118
  108.8 9.8 custom-call.33
  120.1 11.7 %cholesky.431 = f32[128,128]{1,0:T(8,128)S(1)} custom-call(f32[128,128]{1,0:T(8,128)S(1)} %convolution_subtract_fusion.10), custom_call_target="Cholesky" | custom-call | tf_op jit(solution)/shard_map/jit(cholesky)/cholesky | solution.py:118
  138.7 11.7 %while.6 = (s32[]{:T(128)}, f32[512,512]{1,0:T(8,128)}, s32[4,2]{0,1:T(2,128)S(1)}, f32[4,128,128]{2,1,0:T(8,128)S(1)}, s32[]{:T(128)}) while((s32[]{:T(128)}, f32[512,512]{1,0:T(8,128)}, s32[4,2]{0,1:T(2,128)S(1)}, f32[4,128,128]{2,1,0:T(8,128)S(1)}, s32[]{:T(128)}) %tuple.112), condition=%wide.while_cond, body=%wide.while_body.sunk | while | flops 2 | bytes 131189 | solution.py:119
  150.4 39.3 %custom-call.34 = f32[4,128,128]{1,2,0:T(8,128)S(1)} custom-call(f32[4,128,128]{2,1,0:T(8,128)S(1)} %get-tuple-element.31), custom_call_target="InvertDiagBlocksLowerTriangular" | custom-call | tf_op jit(solution)/shard_map/triangular_solve/custom-call.3 | solution.py:119
  196.3 3.7 fusion
  203.7 28.6 %all_to_all.26 = f32[4,128,1024]{2,1,0:T(8,128)S(1)} all-to-all(f32[4,128,1024]{2,1,0:T(8,128)S(1)} %stack.11), channel_id=1, replica_groups=mesh['leaf'=64,'front'=4] {'front'}, dimensions={0} | all-to-all | bytes 4194304 | tf_op jit(solution)/shard_map/all_to_all | solution.py:26
  233.6 3.8 collective-permute-done.2
  241.5 3.1 gather_fusion.3
  245.5 86.4 %collective-permute-done.3 = f32[1024,1024]{1,0:T(8,128)} collective-permute-done((f32[1024,1024]{1,0:T(8,128)}, f32[1024,1024]{1,0:T(8,128)}, u32[]{:S(2)}, u32[]{:S(2)}) %collective-permute-start.3) | collective-permute-done | bytes 4194336 | tf_op jit(solution)/shard_map/ppermute | solution.py:21
  336.7 13.5 %all_to_all.27 = f32[4,96,512]{2,1,0:T(8,128)S(1)} all-to-all(f32[4,96,512]{2,1,0:T(8,128)S(1)} %stack.12), channel_id=1, replica_groups=mesh['leaf'=64,'front'=4] {'front'}, dimensions={0} | all-to-all | bytes 1572864 | tf_op jit(solution)/shard_map/all_to_all | solution.py:26
  356.4 34.2 %collective-permute-done.5 = f32[768,512]{1,0:T(8,128)S(1)} collective-permute-done((f32[768,512]{1,0:T(8,128)S(1)}, f32[768,512]{1,0:T(8,128)S(1)}, u32[]{:S(2)}, u32[]{:S(2)}) %collective-permute-start.5) | collective-permute-done | bytes 1572896 | tf_op jit(solution)/shard_map/ppermute | solution.py:21
  394.8 11.7 %cholesky.446 = f32[128,128]{1,0:T(8,128)S(1)} custom-call(f32[128,128]{1,0:T(8,128)S(1)} %cholesky.599), custom_call_target="Cholesky" | custom-call | tf_op jit(solution)/shard_map/jit(cholesky)/cholesky | solution.py:118
  406.7 9.8 custom-call.35
  419.1 11.7 %cholesky.465 = f32[128,128]{1,0:T(8,128)S(1)} custom-call(f32[128,128]{1,0:T(8,128)S(1)} %cholesky.603), custom_call_target="Cholesky" | custom-call | tf_op jit(solution)/shard_map/jit(cholesky)/cholesky | solution.py:118
  430.8 10.0 custom-call.36
  442.3 11.7 %cholesky.486 = f32[128,128]{1,0:T(8,128)S(1)} custom-call(f32[128,128]{1,0:T(8,128)S(1)} %cholesky.608), custom_call_target="Cholesky" | custom-call | tf_op jit(solution)/shard_map/jit(cholesky)/cholesky | solution.py:118
  454.1 9.8 custom-call.37
  465.4 11.7 %cholesky.503 = f32[128,128]{1,0:T(8,128)S(1)} custom-call(f32[128,128]{1,0:T(8,128)S(1)} %convolution_subtract_fusion.9), custom_call_target="Cholesky" | custom-call | tf_op jit(solution)/shard_map/jit(cholesky)/cholesky | solution.py:118
  483.8 11.8 %while.7 = (s32[]{:T(128)}, f32[512,512]{1,0:T(8,128)}, s32[4,2]{0,1:T(2,128)S(1)}, f32[4,128,128]{2,1,0:T(8,128)S(1)}, s32[]{:T(128)}) while((s32[]{:T(128)}, f32[512,512]{1,0:T(8,128)}, s32[4,2]{0,1:T(2,128)S(1)}, f32[4,128,128]{2,1,0:T(8,128)S(1)}, s32[]{:T(128)}) %tuple.121), condition=%wide.while_cond.clone, body=%wide.while_body.clone.sunk | while | flops 2 | bytes 131189 | solution.py:119
  495.6 39.3 %custom-call.38 = f32[4,128,128]{1,2,0:T(8,128)S(1)} custom-call(f32[4,128,128]{2,1,0:T(8,128)S(1)} %get-tuple-element.32), custom_call_target="InvertDiagBlocksLowerTriangular" | custom-call | tf_op jit(solution)/shard_map/triangular_solve/custom-call.3 | solution.py:119
  541.5 3.7 fusion.6
  548.7 16.4 %all_to_all.28 = f32[4,64,1024]{2,1,0:T(8,128)S(1)} all-to-all(f32[4,64,1024]{2,1,0:T(8,128)S(1)} %stack.13), channel_id=1, replica_groups=mesh['leaf'=64,'front'=4] {'front'}, dimensions={0} | all-to-all | bytes 2097152 | tf_op jit(solution)/shard_map/all_to_all | solution.py:26
  571.7 45.4 %collective-permute-done.7 = f32[512,1024]{1,0:T(8,128)S(1)} collective-permute-done((f32[512,1024]{1,0:T(8,128)S(1)}, f32[512,1024]{1,0:T(8,128)S(1)}, u32[]{:S(2)}, u32[]{:S(2)}) %collective-permute-start.7) | collective-permute-done | bytes 2097184 | tf_op jit(solution)/shard_map/ppermute | solution.py:21
  619.4 3.2 collective-permute-start.8
  626.6 176.1 %collective-permute-done.8 = f32[1024,1024]{1,0:T(8,128)} collective-permute-done((f32[1024,1024]{1,0:T(8,128)}, f32[1024,1024]{1,0:T(8,128)}, u32[]{:S(2)}, u32[]{:S(2)}) %collective-permute-start.8) | collective-permute-done | bytes 4194336 | tf_op jit(solution)/shard_map/ppermute | solution.py:21
  806.8 8.7 all_to_all.29
  821.2 17.3 %collective-permute-done.10 = f32[384,512]{1,0:T(8,128)S(1)} collective-permute-done((f32[384,512]{1,0:T(8,128)S(1)}, f32[384,512]{1,0:T(8,128)S(1)}, u32[]{:S(2)}, u32[]{:S(2)}) %collective-permute-start.10) | collective-permute-done | bytes 786464 | tf_op jit(solution)/shard_map/ppermute | solution.py:21
  838.7 3.7 collective-permute-start.11
  847.9 62.1 %collective-permute-done.11 = f32[768,512]{1,0:T(8,128)S(1)} collective-permute-done((f32[768,512]{1,0:T(8,128)S(1)}, f32[768,512]{1,0:T(8,128)S(1)}, u32[]{:S(2)}, u32[]{:S(2)}) %collective-permute-start.11) | collective-permute-done | bytes 1572896 | tf_op jit(solution)/shard_map/ppermute | solution.py:21
  914.4 11.7 %cholesky.518 = f32[128,128]{1,0:T(8,128)S(1)} custom-call(f32[128,128]{1,0:T(8,128)S(1)} %cholesky.612), custom_call_target="Cholesky" | custom-call | tf_op jit(solution)/shard_map/jit(cholesky)/cholesky | solution.py:118
  926.2 9.8 custom-call.39
  938.6 11.7 %cholesky.537 = f32[128,128]{1,0:T(8,128)S(1)} custom-call(f32[128,128]{1,0:T(8,128)S(1)} %cholesky.616), custom_call_target="Cholesky" | custom-call | tf_op jit(solution)/shard_map/jit(cholesky)/cholesky | solution.py:118
  950.3 10.0 custom-call.40
  961.9 11.7 %cholesky.558 = f32[128,128]{1,0:T(8,128)S(1)} custom-call(f32[128,128]{1,0:T(8,128)S(1)} %cholesky.621), custom_call_target="Cholesky" | custom-call | tf_op jit(solution)/shard_map/jit(cholesky)/cholesky | solution.py:118
  973.6 9.8 custom-call.41
  984.9 12.0 %cholesky.575 = f32[128,128]{1,0:T(8,128)S(1)} custom-call(f32[128,128]{1,0:T(8,128)S(1)} %convolution_subtract_fusion.8), custom_call_target="Cholesky" | custom-call | tf_op jit(solution)/shard_map/jit(cholesky)/cholesky | solution.py:118
  1003.7 11.5 %while.8 = (s32[]{:T(128)}, f32[512,512]{1,0:T(8,128)}, s32[4,2]{0,1:T(2,128)S(1)}, f32[4,128,128]{2,1,0:T(8,128)S(1)}, s32[]{:T(128)}) while((s32[]{:T(128)}, f32[512,512]{1,0:T(8,128)}, s32[4,2]{0,1:T(2,128)S(1)}, f32[4,128,128]{2,1,0:T(8,128)S(1)}, s32[]{:T(128)}) %tuple.122), condition=%wide.while_cond.clone.1, body=%wide.while_body.clone.1.sunk | while | flops 2 | bytes 131189 | solution.py:119
  1015.2 39.3 %custom-call.42 = f32[4,128,128]{1,2,0:T(8,128)S(1)} custom-call(f32[4,128,128]{2,1,0:T(8,128)S(1)} %get-tuple-element.33), custom_call_target="InvertDiagBlocksLowerTriangular" | custom-call | tf_op jit(solution)/shard_map/triangular_solve/custom-call.3 | solution.py:119
  1061.0 3.6 fusion.12
  (249 shorter events, 163.1 us)
Async XLA Ops:
  0.6 10.5 collective-permute-start
  14.9 1.1 copy-start.6
  14.9 1.2 copy-start.8
  17.3 23.1 %copy-start.3 = (f32[192,1536]{1,0:T(8,128)}, f32[192,1536]{1,0:T(8,128)S(1)}, u32[]{:S(2)}) copy-start(f32[192,1536]{1,0:T(8,128)S(1)} %bitcast_add_fusion) | copy-start | bytes 3538948
  40.4 4.5 collective-permute-start.1
  48.3 1.0 copy-start
  200.9 2.7 copy-start.4
  232.3 5.2 collective-permute-start.2
  239.8 92.1 %collective-permute-start.3 = (f32[1024,1024]{1,0:T(8,128)}, f32[1024,1024]{1,0:T(8,128)}, u32[]{:S(2)}, u32[]{:S(2)}) collective-permute-start(f32[1024,1024]{1,0:T(8,128)} %maximum_select_fusion), channel_id=1, source_target_pairs={{0,8},{8,0},{4,12},{12,4},{16,24},{24,16},{20,28},{28,20},{32,40},... | collective-permute-start | bytes 12582920 | tf_op jit(solution)/shard_map/ppermute | solution.py:21
  335.0 1.0 copy-start.7
  335.0 1.0 copy-start.10
  336.6 15.8 %copy-start.5 = (f32[96,1536]{1,0:T(8,128)}, f32[96,1536]{1,0:T(8,128)S(1)}, u32[]{:S(2)}) copy-start(f32[96,1536]{1,0:T(8,128)S(1)} %bitcast_add_fusion.5) | copy-start | bytes 1769476
  350.2 4.0 collective-permute-start.4
  354.4 36.1 %collective-permute-start.5 = (f32[768,512]{1,0:T(8,128)S(1)}, f32[768,512]{1,0:T(8,128)S(1)}, u32[]{:S(2)}, u32[]{:S(2)}) collective-permute-start(f32[768,512]{1,0:T(8,128)S(1)} %maximum_select_fusion.6), channel_id=1, source_target_pairs={{0,8},{8,0},{4,12},{12,4},{16,24},{24,16},{20,28},{28,20},{32,40},... | collective-permute-start | bytes 4718600 | tf_op jit(solution)/shard_map/ppermute | solution.py:21
  393.8 1.0 copy-start.1
  565.1 4.8 collective-permute-start.6
  570.1 52.5 %copy-start.12 = (s32[16,8]{0,1:T(8,128)S(1)}, s32[16,8]{0,1:T(8,128)}, u32[]{:S(2)}) copy-start(s32[16,8]{0,1:T(8,128)} %param.28) | copy-start | bytes 1540
  570.1 46.9 %collective-permute-start.7 = (f32[512,1024]{1,0:T(8,128)S(1)}, f32[512,1024]{1,0:T(8,128)S(1)}, u32[]{:S(2)}, u32[]{:S(2)}) collective-permute-start(f32[512,1024]{1,0:T(8,128)S(1)} %maximum_select_fusion.5), channel_id=1, source_target_pairs={{0,8},{8,0},{4,12},{12,4},{16,24},{24,16},{20,28},{28,20},{32,40},... | collective-permute-start | bytes 6291464 | tf_op jit(solution)/shard_map/ppermute | solution.py:21
  619.4 183.4 %collective-permute-start.8 = (f32[1024,1024]{1,0:T(8,128)}, f32[1024,1024]{1,0:T(8,128)}, u32[]{:S(2)}, u32[]{:S(2)}) collective-permute-start(f32[1024,1024]{1,0:T(8,128)} %maximum_select_fusion.1), channel_id=1, source_target_pairs={{0,16},{16,0},{4,20},{20,4},{8,24},{24,8},{12,28},{28,12},{32,48},... | collective-permute-start | bytes 12582920 | tf_op jit(solution)/shard_map/ppermute | solution.py:21
  805.7 0.9 copy-start.9
  805.7 1.0 copy-start.11
  815.5 4.1 collective-permute-start.9
  819.6 18.9 %collective-permute-start.10 = (f32[384,512]{1,0:T(8,128)S(1)}, f32[384,512]{1,0:T(8,128)S(1)}, u32[]{:S(2)}, u32[]{:S(2)}) collective-permute-start(f32[384,512]{1,0:T(8,128)S(1)} %maximum_select_fusion.8), channel_id=1, source_target_pairs={{0,8},{8,0},{4,12},{12,4},{16,24},{24,16},{20,28},{28,20},{32,40},... | collective-permute-start | bytes 2359304 | tf_op jit(solution)/shard_map/ppermute | solution.py:21
  838.7 71.4 %collective-permute-start.11 = (f32[768,512]{1,0:T(8,128)S(1)}, f32[768,512]{1,0:T(8,128)S(1)}, u32[]{:S(2)}, u32[]{:S(2)}) collective-permute-start(f32[768,512]{1,0:T(8,128)S(1)} %maximum_select_fusion.7), channel_id=1, source_target_pairs={{0,16},{16,0},{4,20},{20,4},{8,24},{24,8},{12,28},{28,12},{32,48},... | collective-permute-start | bytes 4718600 | tf_op jit(solution)/shard_map/ppermute | solution.py:21
  913.4 1.0 copy-start.2
